TPU v7x, 256 devices: a whole 4x4x8 slice. The times are simulated.
256 devices in a mesh: dp: 64 (over z_hi, y, x), mp: 4 (over z_lo, core).
Axes of the slice: x: 4, y: 4, z: 8 (z_hi: 4, z_lo: 2; z = z_hi * 2 + z_lo), core: 2. Of those that a mesh axis runs over, the one named last changes fastest.
Arguments:
- hidden: bfloat16 [2048, 16, 2048], P('dp', None, 'mp'), may hold values from -6 to 6
- norm_gain: bfloat16 [2048], P('mp'), may hold values from 0.099609375 to 1.8984375
- in_x: bfloat16 [2048, 4096], P('dp', 'mp'), may hold values from -0.125 to 0.125
- in_z: bfloat16 [2048, 4096], P('dp', 'mp'), may hold values from -0.125 to 0.125
- conv_weight: float32 [4, 4096], P(None, 'mp'), may hold values from -3 to 3
- conv_bias: float32 [4096], P('mp'), may hold values from -3 to 3
- x_proj: bfloat16 [4096, 160], P(('mp', 'dp')), may hold values from -0.09375 to 0.09375
- dt_proj: bfloat16 [128, 4096], P('dp', 'mp'), may hold values from -0.5 to 0.5
- dt_bias: float32 [4096], P('mp'), may hold values from -5 to -1
- a_log: float32 [16, 4096], P(None, 'mp'), may hold values from 0 to 2.77
- skip: float32 [4096], P('mp'), may hold values from 0.5 to 1.5
- out_proj: bfloat16 [4096, 2048], P('mp', 'dp'), may hold values from -0.09375 to 0.09375
- state_pool: float32 [2560, 16, 4096], P('dp', None, 'mp'), may hold values from -6 to 6
- conv_pool: float32 [2560, 3, 4096], P('dp', None, 'mp'), may hold values from -6 to 6
- permutation: int32 [2048], P('dp'), may hold values from 0 to 2047, as said below
- page_table: int32 [2048], P('dp'), may hold values from 0 to 2559, as said below
- accepted: int32 [2048], P('dp'), may hold values from 1 to 16
Outputs:
- verified: bfloat16 [2048, 16, 2048], P('dp', None, 'mp')
- new_state_pool: float32 [2560, 16, 4096], P('dp', None, 'mp')
- new_conv_pool: float32 [2560, 3, 4096], P('dp', None, 'mp')
Inputs may be any that keep to these rules, and one draw needn't show every extreme that they name: `permutation`: A request at position j of the block of dp index d goes to position j of the block of dp index (d + o) mod 64, where the shift o depends only on j mod 32 and takes 32 different values; so each dp index sends exactly 1 request to each of 32 dp indices and receives 32. `page_table`: the requests of dp index d use distinct slots among the 40 slots d * 40 .. (d + 1) * 40 - 1.
All inputs are finite; a program needn't handle non-finite values.
Results may differ from a plain program's by a relative error of at most 0.0065.
Values may be sent and summed in bfloat16 or wider, within the bound.
No kernel may reach another device: no remote copies, remote signals or barrier semaphores. Data moves between devices by JAX's collectives and lax.ppermute only.
A program may use at most 128 MiB of HBM per device.

v0:
```python
import jax
import jax.numpy as jnp
from jax import lax
from jax.sharding import PartitionSpec as P

EPS = 1e-05


def route_plan(permutation, count, peers):
    capacity = count // min(count, peers)
    target = permutation // count
    order = jnp.arange(count)
    earlier = (target[:, None] == target[None, :]) & (order[None, :] < order[:, None])
    rank_within = jnp.sum(earlier.astype(jnp.int32), axis=1)
    position = target * capacity + rank_within
    match = position[None, :] == jnp.arange(peers * capacity)[:, None]
    filled = jnp.any(match, axis=1)
    source = jnp.argmax(match, axis=1)
    return (position, filled, source)


def pack_rows(values, filled, source):
    picked = jnp.take(values, source, axis=0)
    shape = (filled.shape[0],) + (1,) * (values.ndim - 1)
    return jnp.where(filled.reshape(shape), picked, jnp.zeros_like(picked))


def unpack_rows(values, arrived, count):
    match = arrived[None, :] == jnp.arange(count)[:, None]
    index = jnp.argmax(match, axis=1)
    return jnp.take(values, index, axis=0)


def write_pool(pool, slot_local, values):
    match = slot_local[None, :] == jnp.arange(pool.shape[0])[:, None]
    filled = jnp.any(match, axis=1)
    index = jnp.argmax(match, axis=1)
    return jnp.where(filled[:, None, None], jnp.take(values, index, axis=0), pool)


def verify_layer(
    hidden,
    norm_gain,
    in_x,
    in_z,
    conv_weight,
    conv_bias,
    x_proj,
    dt_proj,
    dt_bias,
    a_log,
    skip,
    out_proj,
    caches,
    accepted,
):
    count, drafts, width_local = hidden.shape
    tokens = count * drafts
    inner_local = in_x.shape[1]
    state_count = a_log.shape[0]
    taps = conv_weight.shape[0]
    rank = x_proj.shape[1] - 2 * state_count
    full, gain_full = (
        lax.all_gather(hidden, "mp", axis=2, tiled=True),
        lax.all_gather(norm_gain, "mp", axis=0, tiled=True),
    )
    rows = full.reshape(tokens, -1).astype(jnp.float32)
    scale = lax.rsqrt(jnp.mean(rows * rows, axis=1, keepdims=True) + EPS)
    normed = (rows * scale * gain_full.astype(jnp.float32)).astype(jnp.bfloat16)
    columns = normed
    x_wide = jnp.dot(
        columns, lax.all_gather(in_x, "dp", axis=0, tiled=True), preferred_element_type=jnp.float32
    )
    z_wide = jnp.dot(
        columns, lax.all_gather(in_z, "dp", axis=0, tiled=True), preferred_element_type=jnp.float32
    )
    x_part = x_wide.astype(jnp.bfloat16)
    z_part = z_wide.astype(jnp.bfloat16)
    states = caches[:, :state_count, :]
    edges = caches[:, state_count:, :]
    padded = jnp.concatenate(
        [edges, x_part.astype(jnp.float32).reshape(count, drafts, inner_local)], axis=1
    )
    mixed = conv_bias + jnp.zeros((count, drafts, inner_local), jnp.float32)
    for offset in range(taps):
        mixed = mixed + conv_weight[offset] * padded[:, offset : offset + drafts, :]
    inputs = jax.nn.silu(mixed).astype(jnp.bfloat16)
    flat_inputs = inputs.reshape(tokens, inner_local)
    piece = lax.all_gather(x_proj, "dp", axis=0, tiled=True)
    columns = flat_inputs
    low_sum = jnp.dot(columns, piece[:, :rank], preferred_element_type=jnp.float32)
    both_sum = jnp.einsum("ks,tk->st", piece[:, rank:], columns, preferred_element_type=jnp.float32)
    low_full, both = lax.psum((low_sum, both_sum), "mp")
    low_half = low_full.astype(jnp.bfloat16)
    columns = low_half
    delta = jnp.dot(
        columns,
        lax.all_gather(dt_proj, "dp", axis=0, tiled=True),
        preferred_element_type=jnp.float32,
    )
    delta = jax.nn.softplus(delta + dt_bias).reshape(count, drafts, inner_local)
    decay_rate = -jnp.exp(a_log)
    inputs_wide = inputs.astype(jnp.float32)
    driven = delta * inputs_wide
    b_time = both[:state_count].reshape(state_count, count, drafts).transpose(2, 1, 0)
    c_time = both[state_count:].reshape(state_count, count, drafts).transpose(2, 1, 0)

    def advance(carry, slices):
        state, kept = carry
        step_delta, step_drive, step_b, step_c, index = slices
        state = (
            jnp.exp(step_delta[:, None, :] * decay_rate[None]) * state
            + step_drive[:, None, :] * step_b[:, :, None]
        )
        output = jnp.sum(state * step_c[:, :, None], axis=1)
        kept = jnp.where((accepted - 1 == index)[:, None, None], state, kept)
        return ((state, kept), output)

    (final_state, kept), outputs = lax.scan(
        advance,
        (states, states),
        (
            delta.transpose(1, 0, 2),
            driven.transpose(1, 0, 2),
            b_time,
            c_time,
            jnp.arange(drafts, dtype=jnp.int32),
        ),
    )
    outputs = outputs.transpose(1, 0, 2)
    gate_wide = z_part.astype(jnp.float32).reshape(count, drafts, inner_local)
    gated = (
        ((outputs + skip * inputs_wide) * jax.nn.silu(gate_wide))
        .astype(jnp.bfloat16)
        .reshape(tokens, inner_local)
    )
    index = accepted[:, None] + jnp.arange(taps - 1, dtype=jnp.int32)[None, :]
    new_edges = jnp.take_along_axis(padded, index[:, :, None], axis=1)
    new_caches = jnp.concatenate([kept, new_edges], axis=1)
    terms = jnp.dot(
        gated,
        lax.all_gather(out_proj, "dp", axis=1, tiled=True),
        preferred_element_type=jnp.float32,
    )
    summed = lax.psum_scatter(terms, "mp", scatter_dimension=1, tiled=True)
    result = (summed + hidden.reshape(tokens, width_local).astype(jnp.float32)).astype(jnp.bfloat16)
    return (result.reshape(count, drafts, width_local), new_caches)


def on_device(
    hidden,
    norm_gain,
    in_x,
    in_z,
    conv_weight,
    conv_bias,
    x_proj,
    dt_proj,
    dt_bias,
    a_log,
    skip,
    out_proj,
    state_pool,
    conv_pool,
    permutation,
    page_table,
    accepted,
):
    count = hidden.shape[0]
    state_count = state_pool.shape[1]
    pool_count = state_pool.shape[0]
    peers = lax.axis_size("dp")
    slot_local = page_table % pool_count
    caches = jnp.concatenate(
        [jnp.take(state_pool, slot_local, axis=0), jnp.take(conv_pool, slot_local, axis=0)], axis=1
    )
    position, filled, source = route_plan(permutation, count, peers)
    arrival_slot = permutation % count
    details = jnp.stack([arrival_slot, accepted], axis=1).astype(jnp.float32)
    details_sent = jnp.where(filled[:, None], jnp.take(details, source, axis=0), -1.0)
    got_hidden = lax.all_to_all(
        pack_rows(hidden, filled, source), "dp", split_axis=0, concat_axis=0, tiled=True
    )
    got_caches, got_details = (
        lax.all_to_all(
            pack_rows(caches, filled, source), "dp", split_axis=0, concat_axis=0, tiled=True
        ),
        lax.all_to_all(details_sent, "dp", split_axis=0, concat_axis=0, tiled=True),
    )
    arrived = got_details[:, 0].astype(jnp.int32)
    local_hidden = unpack_rows(got_hidden, arrived, count)
    local_caches = unpack_rows(got_caches, arrived, count)
    local_accept = unpack_rows(got_details[:, 1], arrived, count).astype(jnp.int32)
    verified, new_caches = verify_layer(
        local_hidden,
        norm_gain,
        in_x,
        in_z,
        conv_weight,
        conv_bias,
        x_proj,
        dt_proj,
        dt_bias,
        a_log,
        skip,
        out_proj,
        local_caches,
        local_accept,
    )
    returned = jnp.take(new_caches, jnp.maximum(arrived, 0), axis=0)
    returned = jnp.where((arrived >= 0)[:, None, None], returned, jnp.zeros_like(returned))
    back = lax.all_to_all(
        returned.astype(jnp.bfloat16), "dp", split_axis=0, concat_axis=0, tiled=True
    ).astype(returned.dtype)
    settled = jnp.take(back, position, axis=0)
    new_state_pool = write_pool(state_pool, slot_local, settled[:, :state_count])
    new_conv_pool = write_pool(conv_pool, slot_local, settled[:, state_count:])
    return (verified, new_state_pool, new_conv_pool)


def solution(mesh):
    return jax.shard_map(
        on_device,
        mesh=mesh,
        in_specs=(
            P("dp", None, "mp"),
            P("mp"),
            P("dp", "mp"),
            P("dp", "mp"),
            P(None, "mp"),
            P("mp"),
            P(("mp", "dp"), None),
            P("dp", "mp"),
            P("mp"),
            P(None, "mp"),
            P("mp"),
            P("mp", "dp"),
            P("dp", None, "mp"),
            P("dp", None, "mp"),
            P("dp"),
            P("dp"),
            P("dp"),
        ),
        out_specs=(P("dp", None, "mp"), P("dp", None, "mp"), P("dp", None, "mp")),
        check_vma=False,
    )
```

profile of v0, /device:TPU:1, one launch (start us, length us, event | category | flops | bytes accessed | tf_op | source)
XLA Modules:
  0.0 935.4 jit_solution(18091020469888556631)
XLA Ops:
  11.0 15.1 %all-to-all-start.1 = ((f32[64,1,2]{2,1,0:T(1,128)}), f32[64,1,2]{2,1,0:T(1,128)S(1)}, u32[]{:S(2)}, u32[]{:S(2)}) async-start(f32[64,1,2]{2,1,0:T(1,128)} %copy.94), calls=%async_computation.1 | async-start | bytes 65536 | tf_op jit(solution)/shard_map/all_to_all | solution.py:188
  27.9 8.8 all-to-all-done.1
  36.7 5.5 all-to-all-start.2
  43.8 23.7 %all-to-all-done.2 = bf16[64,16,512]{2,1,0:T(8,128)(2,1)} async-done(((bf16[64,16,512]{2,1,0:T(8,128)(2,1)}), bf16[64,16,512]{2,1,0:T(8,128)(2,1)}, u32[]{:S(2)}, u32[]{:S(2)}) %all-to-all-start.2) | async-done | bytes 1048608 | tf_op jit(solution)/shard_map/all_to_all | solution.py:181
  67.5 2.6 gather_fusion.4
  70.1 2.0 broadcast_select_fusion.4
  73.4 2.0 gather_fusion
  77.5 3.6 gather_fusion.9
  81.1 7.0 select_select_fusion.1
  88.2 10.0 %all-to-all-start = ((f32[64,19,1024]{2,1,0:T(8,128)}), f32[64,19,1024]{2,1,0:T(8,128)}, u32[]{:S(2)}, u32[]{:S(2)}) async-start(f32[64,19,1024]{2,1,0:T(8,128)} %select_select_fusion.1), calls=%async_computation | async-start | bytes 12582912 | tf_op jit(solution)/shard_map/all_to_all | solution.py:185
  99.0 141.4 %all-gather = bf16[4,1,512]{2,1,0:T(2,128)(2,1)S(1)} all-gather(bf16[1,1,512]{2,1,0:T(2,128)(2,1)S(1)} %reshape.371), channel_id=1, replica_groups=mesh['dp'=64,'mp'=4] {'mp'}, dimensions={0}, use_global_device_ids=true | all-gather | bytes 5120 | tf_op jit(solution)/shard_map/all_gather | solution.py:65
  240.4 184.1 %all_gather.24 = bf16[1024,160]{1,0:T(8,128)(2,1)} all-gather(bf16[16,160]{1,0:T(8,128)(2,1)S(1)} %copy-done.16), channel_id=1, replica_groups=mesh['dp'=64,'mp'=4] {'dp'}, dimensions={0}, use_global_device_ids=true | all-gather | bytes 332800 | tf_op jit(solution)/shard_map/all_gather | solution.py:89
  424.6 2.2 multiply_reduce_fusion.1
  426.9 1.9 fusion.2
  428.8 5.2 convolution_convert_fusion.1
  434.2 5.2 gather_fusion.10
  439.5 2.3 broadcast_select_fusion.2
  443.4 1.4 copy-done.4
  444.9 2.6 multiply_convert_fusion
  447.5 2.0 copy.100
  451.2 160.2 %all-gather.1 = bf16[64,2,1024]{2,1,0:T(2,128)(2,1)S(1)} all-gather(bf16[1,2,1024]{2,1,0:T(2,128)(2,1)S(1)} %bitcast.97), channel_id=1, replica_groups=mesh['dp'=64,'mp'=4] {'dp'}, dimensions={0}, use_global_device_ids=true | all-gather | bytes 266240 | tf_op jit(solution)/shard_map/all_gather | solution.py:98
  612.2 4.5 convolution_convert_fusion
  616.8 1.6 convert.4
  619.9 68.9 %all-reduce.4 = bf16[512,128]{1,0:T(8,128)(2,1)} all-reduce(f32[512,128]{1,0:T(8,128)S(1)} %fusion.12), channel_id=1, replica_groups=mesh['dp'=64,'mp'=4] {'mp'}, use_global_device_ids=true, to_apply=%region_5.8 | all-reduce | flops 65536 | bytes 393216 | tf_op jit(solution)/shard_map/psum | solution.py:93
  688.8 2.3 compare_select_fusion
  691.1 4.6 fusion.3
  698.7 82.8 %while.16 = (s32[]{:T(128)}, f32[32,16,1024]{2,1,0:T(8,128)S(1)}, bf16[32,16,1024]{2,1,0:T(8,128)(2,1)S(1)}, f32[16,32,1024]{2,1,0:T(8,128)}, f32[16,32,1024]{2,...) while((s32[]{:T(128)}, f32[32,16,1024]{2,1,0:T(8,128)S(1)}, ...), condition=%wide.region_9.12_spmd, body=%wide.region_7.11_spmd.sunk | while | flops 3637314 | bytes 9646925 | solution.py:119
  700.5 1.2 multiply_reduce_fusion.3
  710.8 1.2 multiply_reduce_fusion.3
  716.0 1.2 multiply_reduce_fusion.3
  721.1 1.2 multiply_reduce_fusion.3
  726.3 1.2 multiply_reduce_fusion.3
  736.7 1.2 multiply_reduce_fusion.3
  741.8 1.2 multiply_reduce_fusion.3
  781.5 4.1 fusion.6
  786.3 6.6 fusion.29
  794.4 3.3 gather_fusion.8
  798.5 2.4 gather_fusion.11
  800.8 5.5 fusion
  806.4 5.1 all-to-all-start.3
  811.8 94.2 %all-to-all-done.3 = bf16[64,19,1024]{2,1,0:T(8,128)(2,1)S(1)} async-done(((bf16[64,19,1024]{2,1,0:T(8,128)(2,1)}), bf16[64,19,1024]{2,1,0:T(8,128)(2,1)S(1)}, u32[]{:S(2)}, u32[]{:S(2)}) %all-to-all-start.3) | async-done | bytes 2490400 | tf_op jit(solution)/shard_map/all_to_all | solution.py:212
  905.9 3.4 convert_element_type.91
  909.3 3.5 gather_fusion.12
  914.5 2.2 gather_fusion.6
  916.7 3.0 gather_fusion.7
  919.7 1.5 copy_select_fusion
  922.3 3.7 select_select_fusion.2
  926.0 2.3 add_convert_fusion
  (252 shorter events, 99.5 us)
Async XLA Ops:
  7.2 18.9 %copy-start = (bf16[32,16,512]{2,1,0:T(8,128)(2,1)S(1)}, bf16[32,16,512]{2,1,0:T(8,128)(2,1)}, u32[]{:S(2)}) copy-start(bf16[32,16,512]{2,1,0:T(8,128)(2,1)} %param.23) | copy-start | bytes 1572868
  8.1 19.8 %copy-start.21 = (s32[32]{0:T(128)}, s32[32]{0:T(128)S(1)}, u32[]{:S(2)}) copy-start(s32[32]{0:T(128)S(1)} %get-tuple-element.243) | copy-start | bytes 388
  11.0 25.8 %all-to-all-start.1 = ((f32[64,1,2]{2,1,0:T(1,128)}), f32[64,1,2]{2,1,0:T(1,128)S(1)}, u32[]{:S(2)}, u32[]{:S(2)}) async-start(f32[64,1,2]{2,1,0:T(1,128)} %copy.94), calls=%async_computation.1 | async-start | bytes 65536 | tf_op jit(solution)/shard_map/all_to_all | solution.py:188
  36.7 30.7 %all-to-all-start.2 = ((bf16[64,16,512]{2,1,0:T(8,128)(2,1)}), bf16[64,16,512]{2,1,0:T(8,128)(2,1)}, u32[]{:S(2)}, u32[]{:S(2)}) async-start(bf16[64,16,512]{2,1,0:T(8,128)(2,1)} %select_select_fusion.3), calls=%async_computation.2 | async-start | bytes 2097152 | tf_op jit(solution)/shard_map/all_to_all | solution.py:181
  42.3 30.6 %copy-start.24 = (s32[32]{0:T(128)S(1)}, s32[32]{0:T(128)}, u32[]{:S(2)}) copy-start(s32[32]{0:T(128)} %param.38) | copy-start | bytes 388
  42.3 31.1 %copy-start.8 = (f32[40,16,1024]{2,1,0:T(8,128)S(1)}, f32[40,16,1024]{2,1,0:T(8,128)}, u32[]{:S(2)}) copy-start(f32[40,16,1024]{2,1,0:T(8,128)} %param.35) | copy-start | bytes 7864324
  42.3 382.3 %all-gather.7.cloned.1.call-start = ((), (), s32[]{:S(2)}) async-start(), calls=%async_computation.5 | async-start | bytes 2621440 | tf_op jit(solution)/shard_map/all_gather | solution.py:64
  72.1 356.7 %all-gather.9.cloned.1.call-start = ((), (), s32[]{:S(2)}) async-start(), calls=%async_computation.6 | async-start | bytes 4259840 | tf_op jit(solution)/shard_map/all_gather | solution.py:72
  72.8 0.5 copy-start.25
  73.4 2.0 copy-start.2
  75.4 1.6 copy-start.10
  88.2 10.8 %copy-start.20 = (bf16[512]{0:T(512)(128)(2,1)S(1)}, bf16[512]{0:T(512)(128)(2,1)}, u32[]{:S(2)}) copy-start(bf16[512]{0:T(512)(128)(2,1)} %param.24) | copy-start | bytes 3076
  88.2 152.3 %copy-start.16 = (bf16[16,160]{1,0:T(8,128)(2,1)S(1)}, bf16[16,160]{1,0:T(8,128)(2,1)}, u32[]{:S(2)}) copy-start(bf16[16,160]{1,0:T(8,128)(2,1)} %param.29) | copy-start | bytes 15364
  88.2 336.4 %copy-start.15 = (f32[4,1024]{1,0:T(4,128)S(1)}, f32[4,1024]{1,0:T(4,128)}, u32[]{:S(2)}) copy-start(f32[4,1024]{1,0:T(4,128)} %param.27) | copy-start | bytes 49156
  88.2 346.0 %all-to-all-start = ((f32[64,19,1024]{2,1,0:T(8,128)}), f32[64,19,1024]{2,1,0:T(8,128)}, u32[]{:S(2)}, u32[]{:S(2)}) async-start(f32[64,19,1024]{2,1,0:T(8,128)} %select_select_fusion.1), calls=%async_computation | async-start | bytes 12582912 | tf_op jit(solution)/shard_map/all_to_all | solution.py:185
  98.2 514.0 %all-gather.11.cloned.1.call-start = ((), (), s32[]{:S(2)}) async-start(), calls=%async_computation.8 | async-start | bytes 4259840 | tf_op jit(solution)/shard_map/all_gather | solution.py:75
  98.9 596.8 %all-reduce.3.cloned.1.call-start = ((), (), s32[]{:S(2)}) async-start(), calls=%async_computation.7 | async-start | bytes 131072 | tf_op jit(solution)/shard_map/psum | solution.py:93
  424.6 2.3 copy-start.9
  441.7 1.7 copy-start.5
  442.1 2.8 copy-start.17
  443.4 1.4 copy-start.4
  444.9 4.6 copy-start.12
  447.5 3.7 copy-start.18
  447.5 164.7 %copy-start.14 = (f32[16,1024]{1,0:T(8,128)S(1)}, f32[16,1024]{1,0:T(8,128)}, u32[]{:S(2)}) copy-start(f32[16,1024]{1,0:T(8,128)} %param.32) | copy-start | bytes 196612
  447.5 164.7 %copy-start.11 = (bf16[512,2048]{1,0:T(8,128)(2,1)S(1)}, bf16[512,2048]{1,0:T(8,128)(2,1)}, u32[]{:S(2)}) copy-start(bf16[512,2048]{1,0:T(8,128)(2,1)} %fusion.2) | copy-start | bytes 6291460
  450.5 335.8 %all-gather.13.cloned.1.call-start = ((), (), s32[]{:S(2)}) async-start(), calls=%async_computation.9 | async-start | bytes 4259840 | tf_op jit(solution)/shard_map/all_gather | solution.py:142
  451.1 474.9 %reduce-scatter.2.cloned.1.call-start = ((), (), s32[]{:S(2)}) async-start(), calls=%async_computation.10 | async-start | bytes 5242880 | tf_op jit(solution)/shard_map/reduce_scatter | solution.py:145
  616.7 1.7 copy-start.13
  616.8 2.8 copy-start.6
  619.6 69.2 %copy-start.23 = (f32[1024]{0:T(1024)S(1)}, f32[1024]{0:T(1024)}, u32[]{:S(2)}) copy-start(f32[1024]{0:T(1024)} %param.31) | copy-start | bytes 12292
  698.7 82.8 %copy-start.19 = (f32[1024]{0:T(1024)S(1)}, f32[1024]{0:T(1024)}, u32[]{:S(2)}) copy-start(f32[1024]{0:T(1024)} %param.33) | copy-start | bytes 12292
  792.9 0.6 copy-start.26
  806.4 5.1 copy-start.22
  806.4 99.6 %all-to-all-start.3 = ((bf16[64,19,1024]{2,1,0:T(8,128)(2,1)}), bf16[64,19,1024]{2,1,0:T(8,128)(2,1)S(1)}, u32[]{:S(2)}, u32[]{:S(2)}) async-start(bf16[64,19,1024]{2,1,0:T(8,128)(2,1)} %fusion), calls=%async_computation.4 | async-start | bytes 6291456 | tf_op jit(solution)/shard_map/all_to_all | solution.py:212
  914.5 5.2 copy-start.3
  916.7 5.6 copy-start.7
  922.3 6.0 copy-start.1
Sparse Core Ops, SparseCore 0:
  72.2 72.1 all-gather.6
  147.7 163.9 all-gather.8
  315.0 87.4 all-gather.10
  450.6 61.1 all-reduce.2
  515.5 88.7 all-gather.12
  793.0 89.7 reduce-scatter.1
where the time goes:
time: 945 us; the launch traced here: 935 us
  blocking collectives  555 us (59%)
  waiting for transfers between devices  129 us (14%)
  local copies, waits for them, and re-layouts  94 us (10%)
  other arithmetic  86.5 us (9%)
  starting transfers between devices  36 us (4%)
  matrix products  20.1 us (2%)
  between operations  14.9 us (2%)
    all_gather x1, blocking collectives, verify_layer(): piece = lax.all_gather(x_proj, 'dp', axis=0, tiled=True)  184 us
    all_gather x1, blocking collectives, verify_layer(): lax.all_gather(dt_proj, 'dp', axis=0, tiled=True)  160 us
    all_gather x1, blocking collectives, verify_layer(): lax.all_gather(norm_gain, 'mp', axis=0, tiled=True)  141 us
    all_to_all x1, waiting for transfers between devices, on_device(): lax.all_to_all(returned.astype(jnp.bfloat16), 'dp', split_axis=0, concat_...  94.2 us
    psum x1, blocking collectives, verify_layer(): low_full, both = lax.psum((low_sum, both_sum), 'mp')  68.9 us
    all_to_all x1, waiting for transfers between devices, on_device(): lax.all_to_all(pack_rows(hidden, filled, source), 'dp', split_axis=0, con...  23.7 us
    reduce_sum x16, other arithmetic, advance(): output = jnp.sum(state * step_c[:, :, None], axis=1)  19.9 us
  transfers between devices with their start and end apart: 10, of which 3 were waited for; matrix products, arithmetic and copies ran while one was open for 19% of the time, Pallas kernels for 0%

commit v1 on v0

--- a/solution.py
+++ b/solution.py
@@ -86,7 +86,9 @@
         mixed = mixed + conv_weight[offset] * padded[:, offset : offset + drafts, :]
     inputs = jax.nn.silu(mixed).astype(jnp.bfloat16)
     flat_inputs = inputs.reshape(tokens, inner_local)
-    piece = lax.all_gather(x_proj, "dp", axis=0, tiled=True)
+    piece = jnp.concatenate(
+        lax.all_to_all(jnp.stack([x_proj] * lax.axis_size("dp")), "dp", 0, 0), axis=0
+    )
     columns = flat_inputs
     low_sum = jnp.dot(columns, piece[:, :rank], preferred_element_type=jnp.float32)
     both_sum = jnp.einsum("ks,tk->st", piece[:, rank:], columns, preferred_element_type=jnp.float32)

time: 945 us -> 826 us (0.87)
  blocking collectives: 555 us -> 353 us
  waiting for transfers between devices: 129 us -> 196 us
  starting transfers between devices: 36 us -> 45.8 us
    all_gather x1 -> x0, blocking collectives: 184 us -> none  [verify_layer(): piece = lax.all_gather(x_proj, 'dp', axis=0, tiled=True)]
    all_gather x1, waiting for transfers between devices: 0.01 us -> 66.7 us  [verify_layer(): lax.all_gather(in_x, 'dp', axis=0, tiled=True)]
    psum x1, blocking collectives: 68.9 us -> 42.8 us  [verify_layer(): low_full, both = lax.psum((low_sum, both_sum), 'mp')]
    all_to_all x0 -> x1, starting transfers between devices: none -> 9.52 us  [verify_layer(): lax.all_to_all(jnp.stack([x_proj] * lax.axis_size('dp')), 'dp', 0, 0)]
  transfers between devices with their start and end apart: 10 -> 11, of which waited for: 3 -> 5; matrix products, arithmetic and copies ran while one was open for 19% -> 22% of each run, Pallas kernels for 0% -> 0%
where the time goes in v1:
time: 826 us; the launch traced here: 814 us
  blocking collectives  353 us (43%)
  waiting for transfers between devices  196 us (24%)
  local copies, waits for them, and re-layouts  94.6 us (11%)
  other arithmetic  86.5 us (10%)
  starting transfers between devices  45.8 us (6%)
  matrix products  22.1 us (3%)
  between operations  14.9 us (2%)
    all_gather x1, blocking collectives, verify_layer(): lax.all_gather(dt_proj, 'dp', axis=0, tiled=True)  168 us
    all_gather x1, blocking collectives, verify_layer(): lax.all_gather(norm_gain, 'mp', axis=0, tiled=True)  143 us
    all_to_all x1, waiting for transfers between devices, on_device(): lax.all_to_all(returned.astype(jnp.bfloat16), 'dp', split_axis=0, concat_...  93 us
    all_gather x1, waiting for transfers between devices, verify_layer(): lax.all_gather(in_x, 'dp', axis=0, tiled=True)  66.7 us
    psum x1, blocking collectives, verify_layer(): low_full, both = lax.psum((low_sum, both_sum), 'mp')  42.8 us
    all_to_all x1, waiting for transfers between devices, on_device(): lax.all_to_all(pack_rows(hidden, filled, source), 'dp', split_axis=0, con...  23.7 us
    reduce_sum x16, other arithmetic, advance(): output = jnp.sum(state * step_c[:, :, None], axis=1)  19.9 us
  transfers between devices with their start and end apart: 11, of which 5 were waited for; matrix products, arithmetic and copies ran while one was open for 22% of the time, Pallas kernels for 0%

profile of v1, /device:TPU:1, one launch (start us, length us, event | category | flops | bytes accessed | tf_op | source)
XLA Modules:
  0.0 813.6 jit_solution(725193732523110120)
XLA Ops:
  11.0 15.1 %all-to-all-start.1 = ((f32[64,1,2]{2,1,0:T(1,128)}), f32[64,1,2]{2,1,0:T(1,128)S(1)}, u32[]{:S(2)}, u32[]{:S(2)}) async-start(f32[64,1,2]{2,1,0:T(1,128)} %copy.94), calls=%async_computation.1 | async-start | bytes 65536 | tf_op jit(solution)/shard_map/all_to_all | solution.py:190
  27.9 8.8 %all-to-all-done.1 = f32[64,1,2]{2,1,0:T(1,128)S(1)} async-done(((f32[64,1,2]{2,1,0:T(1,128)}), f32[64,1,2]{2,1,0:T(1,128)S(1)}, u32[]{:S(2)}, u32[]{:S(2)}) %all-to-all-start.1) | async-done | bytes 544 | tf_op jit(solution)/shard_map/all_to_all | solution.py:190
  36.7 5.5 all-to-all-start.2
  43.8 23.7 %all-to-all-done.2 = bf16[64,16,512]{2,1,0:T(8,128)(2,1)} async-done(((bf16[64,16,512]{2,1,0:T(8,128)(2,1)}), bf16[64,16,512]{2,1,0:T(8,128)(2,1)}, u32[]{:S(2)}, u32[]{:S(2)}) %all-to-all-start.2) | async-done | bytes 1048608 | tf_op jit(solution)/shard_map/all_to_all | solution.py:183
  67.5 2.6 gather_fusion.4
  70.1 2.0 broadcast_select_fusion.4
  73.4 2.0 gather_fusion
  77.5 3.6 gather_fusion.9
  81.1 7.0 select_select_fusion.1
  88.2 10.0 %all-to-all-start = ((f32[64,19,1024]{2,1,0:T(8,128)}), f32[64,19,1024]{2,1,0:T(8,128)}, u32[]{:S(2)}, u32[]{:S(2)}) async-start(f32[64,19,1024]{2,1,0:T(8,128)} %select_select_fusion.1), calls=%async_computation | async-start | bytes 12582912 | tf_op jit(solution)/shard_map/all_to_all | solution.py:187
  99.0 142.6 %all-gather = bf16[4,1,512]{2,1,0:T(2,128)(2,1)S(1)} all-gather(bf16[1,1,512]{2,1,0:T(2,128)(2,1)S(1)} %reshape.377), channel_id=1, replica_groups=mesh['dp'=64,'mp'=4] {'mp'}, dimensions={0}, use_global_device_ids=true | all-gather | bytes 5120 | tf_op jit(solution)/shard_map/all_gather | solution.py:65
  241.6 2.2 multiply_reduce_fusion.1
  244.0 1.9 fusion.2
  245.8 66.7 %all-gather.9.cloned.1.call-done = bf16[2048,1024]{1,0:T(8,128)(2,1)} async-done(((bf16[32,1024]{1,0:T(8,128)(2,1)}), bf16[2048,1024]{1,0:T(8,128)(2,1)}) %all-gather.9.cloned.1.call-update) | async-done | bytes 4194320 | tf_op jit(solution)/shard_map/all_gather | solution.py:72
  312.5 5.2 convolution_convert_fusion.1
  319.2 9.5 %all-to-all-start.3 = ((bf16[64,16,160]{2,1,0:T(8,128)(2,1)}), bf16[64,16,160]{2,1,0:T(8,128)(2,1)}, u32[]{:S(2)}, u32[]{:S(2)}) async-start(bf16[64,16,160]{2,1,0:T(8,128)(2,1)} %stack.11), calls=%async_computation.3 | async-start | bytes 1048576 | tf_op jit(solution)/shard_map/all_to_all | solution.py:90
  329.3 5.2 gather_fusion.10
  334.5 2.3 broadcast_select_fusion.2
  338.5 1.4 copy-done.4
  339.9 2.6 multiply_convert_fusion
  342.5 2.0 copy.100
  344.5 1.4 all-to-all-done.3
  345.9 2.0 convolution_bitcast_fusion
  348.5 168.1 %all-gather.1 = bf16[64,2,1024]{2,1,0:T(2,128)(2,1)S(1)} all-gather(bf16[1,2,1024]{2,1,0:T(2,128)(2,1)S(1)} %bitcast.98), channel_id=1, replica_groups=mesh['dp'=64,'mp'=4] {'dp'}, dimensions={0}, use_global_device_ids=true | all-gather | bytes 266240 | tf_op jit(solution)/shard_map/all_gather | solution.py:100
  517.5 4.5 convolution_convert_fusion
  522.0 1.6 convert.4
  523.6 1.5 fusion.12
  525.5 42.8 %all-reduce.4 = bf16[512,128]{1,0:T(8,128)(2,1)} all-reduce(f32[512,128]{1,0:T(8,128)S(1)} %fusion.12), channel_id=1, replica_groups=mesh['dp'=64,'mp'=4] {'mp'}, use_global_device_ids=true, to_apply=%region_5.8 | all-reduce | flops 65536 | bytes 393216 | tf_op jit(solution)/shard_map/psum | solution.py:95
  568.3 2.3 compare_select_fusion
  570.6 4.6 fusion.3
  578.2 82.8 %while.16 = (s32[]{:T(128)}, f32[32,16,1024]{2,1,0:T(8,128)S(1)}, bf16[32,16,1024]{2,1,0:T(8,128)(2,1)S(1)}, f32[16,32,1024]{2,1,0:T(8,128)}, f32[16,32,1024]{2,...) while((s32[]{:T(128)}, f32[32,16,1024]{2,1,0:T(8,128)S(1)}, ...), condition=%wide.region_9.12_spmd, body=%wide.region_7.11_spmd.sunk | while | flops 3637314 | bytes 9646925 | solution.py:121
  590.3 1.2 multiply_reduce_fusion.3
  595.5 1.2 multiply_reduce_fusion.3
  600.7 1.2 multiply_reduce_fusion.3
  661.1 4.1 fusion.6
  665.8 6.6 fusion.29
  673.9 3.3 gather_fusion.8
  678.0 2.4 gather_fusion.11
  680.3 5.5 fusion
  685.9 4.9 all-to-all-start.4
  691.1 93.0 %all-to-all-done.4 = bf16[64,19,1024]{2,1,0:T(8,128)(2,1)S(1)} async-done(((bf16[64,19,1024]{2,1,0:T(8,128)(2,1)}), bf16[64,19,1024]{2,1,0:T(8,128)(2,1)S(1)}, u32[]{:S(2)}, u32[]{:S(2)}) %all-to-all-start.4) | async-done | bytes 2490400 | tf_op jit(solution)/shard_map/all_to_all | solution.py:214
  784.1 3.4 convert_element_type.91
  787.5 3.5 gather_fusion.12
  792.7 2.2 gather_fusion.6
  794.9 3.0 gather_fusion.7
  797.9 1.5 copy_select_fusion
  800.5 3.7 select_select_fusion.2
  804.1 2.3 add_convert_fusion
  (250 shorter events, 104.0 us)
Async XLA Ops:
  7.2 18.9 %copy-start = (bf16[32,16,512]{2,1,0:T(8,128)(2,1)S(1)}, bf16[32,16,512]{2,1,0:T(8,128)(2,1)}, u32[]{:S(2)}) copy-start(bf16[32,16,512]{2,1,0:T(8,128)(2,1)} %param.23) | copy-start | bytes 1572868
  8.1 19.8 %copy-start.19 = (s32[32]{0:T(128)}, s32[32]{0:T(128)S(1)}, u32[]{:S(2)}) copy-start(s32[32]{0:T(128)S(1)} %get-tuple-element.243) | copy-start | bytes 388
  11.0 25.8 %all-to-all-start.1 = ((f32[64,1,2]{2,1,0:T(1,128)}), f32[64,1,2]{2,1,0:T(1,128)S(1)}, u32[]{:S(2)}, u32[]{:S(2)}) async-start(f32[64,1,2]{2,1,0:T(1,128)} %copy.94), calls=%async_computation.1 | async-start | bytes 65536 | tf_op jit(solution)/shard_map/all_to_all | solution.py:190
  36.7 30.7 %all-to-all-start.2 = ((bf16[64,16,512]{2,1,0:T(8,128)(2,1)}), bf16[64,16,512]{2,1,0:T(8,128)(2,1)}, u32[]{:S(2)}, u32[]{:S(2)}) async-start(bf16[64,16,512]{2,1,0:T(8,128)(2,1)} %select_select_fusion.3), calls=%async_computation.2 | async-start | bytes 2097152 | tf_op jit(solution)/shard_map/all_to_all | solution.py:183
  42.3 30.6 %copy-start.22 = (s32[32]{0:T(128)S(1)}, s32[32]{0:T(128)}, u32[]{:S(2)}) copy-start(s32[32]{0:T(128)} %param.38) | copy-start | bytes 388
  42.3 31.1 %copy-start.8 = (f32[40,16,1024]{2,1,0:T(8,128)S(1)}, f32[40,16,1024]{2,1,0:T(8,128)}, u32[]{:S(2)}) copy-start(f32[40,16,1024]{2,1,0:T(8,128)} %param.35) | copy-start | bytes 7864324
  42.3 199.3 %all-gather.7.cloned.1.call-start = ((), (), s32[]{:S(2)}) async-start(), calls=%async_computation.6 | async-start | bytes 2621440 | tf_op jit(solution)/shard_map/all_gather | solution.py:64
  72.1 240.5 %all-gather.9.cloned.1.call-start = ((), (), s32[]{:S(2)}) async-start(), calls=%async_computation.7 | async-start | bytes 4259840 | tf_op jit(solution)/shard_map/all_gather | solution.py:72
  72.8 0.5 copy-start.23
  73.4 2.0 copy-start.2
  75.4 1.6 copy-start.10
  88.2 10.8 %copy-start.18 = (bf16[512]{0:T(512)(128)(2,1)S(1)}, bf16[512]{0:T(512)(128)(2,1)}, u32[]{:S(2)}) copy-start(bf16[512]{0:T(512)(128)(2,1)} %param.24) | copy-start | bytes 3076
  88.2 153.4 %copy-start.13 = (f32[4,1024]{1,0:T(4,128)S(1)}, f32[4,1024]{1,0:T(4,128)}, u32[]{:S(2)}) copy-start(f32[4,1024]{1,0:T(4,128)} %param.27) | copy-start | bytes 49156
  88.2 229.8 %all-to-all-start = ((f32[64,19,1024]{2,1,0:T(8,128)}), f32[64,19,1024]{2,1,0:T(8,128)}, u32[]{:S(2)}, u32[]{:S(2)}) async-start(f32[64,19,1024]{2,1,0:T(8,128)} %select_select_fusion.1), calls=%async_computation | async-start | bytes 12582912 | tf_op jit(solution)/shard_map/all_to_all | solution.py:187
  98.2 419.2 %all-gather.11.cloned.1.call-start = ((), (), s32[]{:S(2)}) async-start(), calls=%async_computation.9 | async-start | bytes 4259840 | tf_op jit(solution)/shard_map/all_gather | solution.py:75
  241.6 2.3 copy-start.9
  317.7 0.7 copy-start.14
  319.2 26.6 %all-to-all-start.3 = ((bf16[64,16,160]{2,1,0:T(8,128)(2,1)}), bf16[64,16,160]{2,1,0:T(8,128)(2,1)}, u32[]{:S(2)}, u32[]{:S(2)}) async-start(bf16[64,16,160]{2,1,0:T(8,128)(2,1)} %stack.11), calls=%async_computation.3 | async-start | bytes 1048576 | tf_op jit(solution)/shard_map/all_to_all | solution.py:90
  328.7 246.5 %all-reduce.3.cloned.1.call-start = ((), (), s32[]{:S(2)}) async-start(), calls=%async_computation.8 | async-start | bytes 131072 | tf_op jit(solution)/shard_map/psum | solution.py:95
  336.8 1.7 copy-start.5
  337.1 2.8 copy-start.15
  338.5 1.4 copy-start.4
  342.5 6.0 copy-start.16
  342.5 174.9 %copy-start.12 = (f32[16,1024]{1,0:T(8,128)S(1)}, f32[16,1024]{1,0:T(8,128)}, u32[]{:S(2)}) copy-start(f32[16,1024]{1,0:T(8,128)} %param.32) | copy-start | bytes 196612
  342.5 175.0 %copy-start.11 = (bf16[512,2048]{1,0:T(8,128)(2,1)S(1)}, bf16[512,2048]{1,0:T(8,128)(2,1)}, u32[]{:S(2)}) copy-start(bf16[512,2048]{1,0:T(8,128)(2,1)} %fusion.2) | copy-start | bytes 6291460
  347.9 317.9 %all-gather.13.cloned.1.call-start = ((), (), s32[]{:S(2)}) async-start(), calls=%async_computation.10 | async-start | bytes 4259840 | tf_op jit(solution)/shard_map/all_gather | solution.py:144
  348.5 455.7 %reduce-scatter.2.cloned.1.call-start = ((), (), s32[]{:S(2)}) async-start(), calls=%async_computation.11 | async-start | bytes 5242880 | tf_op jit(solution)/shard_map/reduce_scatter | solution.py:147
  522.0 3.2 copy-start.6
  525.1 43.2 %copy-start.21 = (f32[1024]{0:T(1024)S(1)}, f32[1024]{0:T(1024)}, u32[]{:S(2)}) copy-start(f32[1024]{0:T(1024)} %param.31) | copy-start | bytes 12292
  578.2 82.8 %copy-start.17 = (f32[1024]{0:T(1024)S(1)}, f32[1024]{0:T(1024)}, u32[]{:S(2)}) copy-start(f32[1024]{0:T(1024)} %param.33) | copy-start | bytes 12292
  672.4 0.6 copy-start.24
  685.9 4.9 copy-start.20
  685.9 98.2 %all-to-all-start.4 = ((bf16[64,19,1024]{2,1,0:T(8,128)(2,1)}), bf16[64,19,1024]{2,1,0:T(8,128)(2,1)S(1)}, u32[]{:S(2)}, u32[]{:S(2)}) async-start(bf16[64,19,1024]{2,1,0:T(8,128)(2,1)} %fusion), calls=%async_computation.5 | async-start | bytes 6291456 | tf_op jit(solution)/shard_map/all_to_all | solution.py:214
  792.7 5.2 copy-start.3
  794.9 5.6 copy-start.7
  800.5 6.0 copy-start.1
Sparse Core Ops, SparseCore 0:
  72.2 72.1 all-gather.6
  147.7 164.7 all-gather.8
  315.8 91.7 all-gather.10
  410.1 39.2 all-reduce.2
  453.1 90.4 all-gather.12
  672.5 87.3 reduce-scatter.1
